TPU v7x, 256 devices: a whole 4x4x8 slice. The times are simulated.
256 devices in a mesh: grp: 8 (over z), feat: 32 (over x, y, core).
Axes of the slice: x: 4, y: 4, z: 8, core: 2. Of those that a mesh axis runs over, the one named last changes fastest.
Arguments:
- features: bfloat16 [65536, 512], P(('grp', 'feat')), may hold values from -6 to 6
- adj_tiles: bfloat16 [512, 16, 128, 128], P(('grp', 'feat')), may hold values from 0.0099487305 to 1
- src_block: int32 [512, 16], P(('grp', 'feat')), may hold values from 0 to 63, as said below
- counts: int32 [512], P(('grp', 'feat')), may hold values from 1 to 16, as said below
- w_self: bfloat16 [512, 512], replicated, may hold values from -0.25 to 0.25
- w_neigh: bfloat16 [512, 512], replicated, may hold values from -0.25 to 0.25
- multiplier: float32 [512], replicated, may hold values from 0.5 to 2
- bit_shift: int32 [512], replicated, may hold values from 0 to 2
- cotangent: bfloat16 [65536, 512], P(('grp', 'feat')), may hold values from -6 to 6
Outputs:
- output: bfloat16 [65536, 512], P(('grp', 'feat'))
- grad_features: bfloat16 [65536, 512], P(('grp', 'feat'))
- grad_self: float32 [512, 512], replicated
- grad_neigh: float32 [512, 512], replicated
Inputs may be any that keep to these rules, and one draw needn't show every extreme that they name: src_block[i, k] is a block of block i's own group, held by a device at most 2 positions from block i's device in the group's cyclic order of devices (block i is held by device (i % 64) // 2 of its group, which holds 2 consecutive blocks); the distance 2 is reached in both directions in every draw. Slots k >= counts[i] take no part.
All inputs are finite; a program needn't handle non-finite values.
Results may differ from a plain program's by a relative error of at most 0.0059.
Values may be sent and summed in bfloat16 or wider, within the bound.
No kernel may reach another device: no remote copies, remote signals or barrier semaphores. Data moves between devices by JAX's collectives and lax.ppermute only.
A program may use at most 64 MiB of HBM per device.

v0:
```python
import math
import jax
import jax.numpy as jnp
from jax import lax
from jax.sharding import PartitionSpec as P

SPAN = 2


def passed_along(x, axis, by):
    peers = lax.axis_size(axis)
    return lax.ppermute(x, axis, [(i, (i + by) % peers) for i in range(peers)])


def fetch_near(shard_piece, steps_by):
    return passed_along(shard_piece, "feat", steps_by)


def return_near(shard_piece, steps_by):
    return passed_along(shard_piece, "feat", steps_by)


def local(
    features, adj_tiles, src_block, counts, w_self, w_neigh, multiplier, bit_shift, cotangent
):
    num_blocks = adj_tiles.shape[0]
    num_slots = adj_tiles.shape[1]
    block_len = adj_tiles.shape[2]
    feature_width = features.shape[1]
    row_count = features.shape[0]
    feat_count = lax.axis_size("feat")
    my_index = lax.axis_index("feat")
    live_mask = jnp.arange(num_slots, dtype=jnp.int32)[None, :] < counts[:, None]
    masked = jnp.where(live_mask[:, :, None, None], adj_tiles, jnp.zeros_like(adj_tiles))
    degree = jnp.sum(masked, axis=(1, 3), dtype=jnp.float32)
    inv_root = lax.rsqrt(degree)
    node_blocks = features.reshape(num_blocks, block_len, feature_width)
    pieces = {0: node_blocks}
    for offset in range(-SPAN, SPAN + 1):
        if offset != 0:
            pieces[offset] = fetch_near(node_blocks, -offset)
    source_pool = jnp.concatenate([pieces[offset] for offset in range(-SPAN, SPAN + 1)], axis=0)
    relative = (src_block // num_blocks - my_index + SPAN) % feat_count
    slot_index = relative * num_blocks + src_block % num_blocks
    flat_index = slot_index.reshape(-1)
    sources = jnp.take(source_pool, flat_index, axis=0).reshape(
        num_blocks, num_slots, block_len, feature_width
    )
    summed = jnp.einsum("bkij,bkjf->bif", masked, sources, preferred_element_type=jnp.float32)
    aggregated = (
        (summed * inv_root[:, :, None]).astype(jnp.bfloat16).reshape(row_count, feature_width)
    )
    preact = jnp.dot(features, w_self, preferred_element_type=jnp.float32)
    preact = preact + jnp.dot(aggregated, w_neigh, preferred_element_type=jnp.float32)
    scale = multiplier * jnp.exp2(-bit_shift.astype(jnp.float32))
    scaled = preact * scale
    sigmoid_val = jax.nn.sigmoid(scaled)
    output = (scaled * sigmoid_val).astype(jnp.bfloat16)
    grad_pre = (
        cotangent.astype(jnp.float32) * sigmoid_val * (1.0 + scaled * (1.0 - sigmoid_val)) * scale
    ).astype(jnp.bfloat16)
    part_self = jnp.dot(features.T, grad_pre, preferred_element_type=jnp.float32)
    part_neigh = jnp.dot(aggregated.T, grad_pre, preferred_element_type=jnp.float32)
    total_self, total_neigh = lax.psum((part_self, part_neigh), ("grp", "feat"))
    grad_scale = 1.0 / math.sqrt(row_count * lax.axis_size("grp") * feat_count)
    own_part = jnp.dot(grad_pre, w_self.T, preferred_element_type=jnp.float32)
    back = jnp.dot(grad_pre, w_neigh.T, preferred_element_type=jnp.float32).reshape(
        num_blocks, block_len, feature_width
    )
    back = (back * inv_root[:, :, None]).astype(jnp.bfloat16)
    contrib = jnp.einsum("bkij,bif->bkjf", masked, back, preferred_element_type=jnp.float32)
    contrib_flat = contrib.reshape(num_blocks * num_slots, block_len * feature_width)
    window_count = (2 * SPAN + 1) * num_blocks
    grouped = jax.ops.segment_sum(contrib_flat, flat_index, num_segments=window_count)
    window = lax.optimization_barrier(grouped.astype(jnp.bfloat16))
    window = window.reshape(window_count, block_len, feature_width)

    def window_piece(offset):
        first_block = (offset + SPAN) * num_blocks
        return window[first_block : first_block + num_blocks]

    spread_blocks = window_piece(0).astype(jnp.float32)
    for offset in range(-SPAN, SPAN + 1):
        if offset != 0:
            arrived = return_near(window_piece(offset), offset)
            spread_blocks = spread_blocks + arrived.astype(jnp.float32)
    spread = spread_blocks.reshape(row_count, feature_width)
    grad_features = (own_part + spread).astype(jnp.bfloat16)
    return (output, grad_features, total_self * grad_scale, total_neigh * grad_scale)


def solution(mesh):
    return jax.shard_map(
        local,
        mesh=mesh,
        in_specs=(
            P(("grp", "feat"), None),
            P(("grp", "feat"), None, None, None),
            P(("grp", "feat"), None),
            P(("grp", "feat")),
            P(),
            P(),
            P(),
            P(),
            P(("grp", "feat"), None),
        ),
        out_specs=(P(("grp", "feat"), None), P(("grp", "feat"), None), P(), P()),
        check_vma=False,
    )
```

profile of v0, /device:TPU:2, one launch (start us, length us, event | category | flops | bytes accessed | tf_op | source)
XLA Modules:
  0.0 402.8 jit_solution(4255000697265647718)
XLA Ops:
  7.2 0.0 copy-start
  7.2 0.0 copy-start.2
  7.2 0.0 all-reduce.3.cloned.1.call-start
  7.2 1.7 collective-permute-start
  8.9 0.0 collective-permute-start.1
  8.9 3.9 collective-permute-start.2
  12.7 0.5 collective-permute-start.3
  13.2 0.7 compare_and_fusion
  13.9 0.1 reshape.97
  14.0 0.7 iota_compare_fusion
  14.7 2.2 fusion.33
  16.9 0.7 exponential_multiply_fusion
  17.6 1.6 convert_reduce_fusion
  19.3 0.1 reshape.113
  19.3 0.0 collective-permute-done
  19.4 1.1 collective-permute-done.1
  20.5 0.0 copy-done.2
  20.5 0.0 collective-permute-done.2
  20.6 1.4 collective-permute-done.3
  22.0 0.0 copy-start.1
  22.0 2.8 gather_fusion
  24.8 3.1 fusion.11
  27.9 1.2 multiply_convert_fusion.1
  29.2 1.3 fusion.35
  30.5 1.3 convolution_bitcast_fusion
  31.8 0.3 fusion.34
  32.1 1.4 fusion.14
  33.5 8.1 %copy.21 = f32[4,8,128,512]{3,1,2,0:T(8,128)} copy(f32[4,8,128,512]{3,2,1,0:T(8,128)S(1)} %bitcast.65) | data formatting | bytes 16777216
  41.6 2.2 broadcast_in_dim.35
  43.9 75.4 %scatter_fusion = f32[10,65536]{1,0:T(8,128)} fusion(f32[10,65536]{1,0:T(8,128)} %broadcast_in_dim.35, s32[32]{0:T(128)S(1)} %reshape.113, f32[32,65536]{1,0:T(8,128)} %bitcast.64), kind=kCustom, calls=%fused_computation.1 | custom fusion | flops 2097152 | bytes 25165952 | tf_op jit(solution)/shard_map/scatter-add | solution.py:74
  119.3 2.4 convert_element_type.52
  121.7 0.0 all-reduce.3.cloned.1.call-update
  121.7 0.8 fusion.32
  122.5 0.0 copy-start.3
  122.6 4.9 %collective-permute-start.4 = (bf16[2,128,512]{2,1,0:T(8,128)(2,1)S(1)}, bf16[2,128,512]{2,1,0:T(8,128)(2,1)S(1)}, u32[]{:S(2)}, u32[]{:S(2)}) collective-permute-start(bf16[2,128,512]{2,1,0:T(8,128)(2,1)S(1)} %bitcast.78), channel_id=1, source_target_pairs={{0,30},{1,31},{2,0},{3,1},{4,2},{5,3},{6,4},{7,5},{8,6},{9,7},{10,... | collective-permute-start | bytes 786440 | tf_op jit(solution)/shard_map/ppermute | solution.py:12
  127.5 0.1 collective-permute-start.5
  127.6 0.6 collective-permute-start.6
  128.2 0.1 collective-permute-start.7
  128.3 3.0 collective-permute-done.4
  131.4 2.8 collective-permute-done.5
  134.2 3.1 collective-permute-done.6
  137.2 2.4 collective-permute-done.7
  139.6 0.2 fusion.17
  139.8 1.0 fusion.18
  140.8 250.7 %all-reduce.3.cloned.1.call-done = (f32[512,512]{0,1:T(8,128)}, f32[512,512]{0,1:T(8,128)}) async-done(((f32[512,512]{0,1:T(8,128)}, f32[512,512]{0,1:T(8,128)}), (f32[512,512]{0,1:T(8,128)}, f32[512,512]{0,1:T(8,128)})) %all-reduce.3.cloned.1.call-update) | async-done | bytes 2097168 | tf_op jit(solution)/shard_map/psum | solution.py:64
  391.5 1.8 broadcast_multiply_fusion
  393.4 1.3 copy.15
  394.7 1.3 copy.16
  (19 shorter events, 0.2 us)
Async XLA Ops:
  7.2 20.8 %copy-start = (bf16[512,512]{1,0:T(8,128)(2,1)S(1)}, bf16[512,512]{1,0:T(8,128)(2,1)}, u32[]{:S(2)}) copy-start(bf16[512,512]{1,0:T(8,128)(2,1)} %param.14) | copy-start | bytes 1572868
  7.2 13.3 %copy-start.2 = (bf16[256,512]{1,0:T(8,128)(2,1)S(1)}, bf16[256,512]{1,0:T(8,128)(2,1)}, u32[]{:S(2)}) copy-start(bf16[256,512]{1,0:T(8,128)(2,1)} %param.9) | copy-start | bytes 786436
  7.2 384.4 %all-reduce.3.cloned.1.call-start = ((), (), s32[]{:S(2)}) async-start(), calls=%async_computation | async-start | bytes 4194304 | tf_op jit(solution)/shard_map/psum | solution.py:64
  7.2 12.1 %collective-permute-start = (bf16[2,128,512]{2,1,0:T(8,128)(2,1)}, bf16[2,128,512]{2,1,0:T(8,128)(2,1)S(1)}, u32[]{:S(2)}, u32[]{:S(2)}) collective-permute-start(bf16[2,128,512]{2,1,0:T(8,128)(2,1)} %bitcast.67), channel_id=1, source_target_pairs={{0,2},{1,3},{2,4},{3,5},{4,6},{5,7},{6,8},{7,9},{8,10},{9,11},{10,... | collective-permute-start | bytes 786440 | tf_op jit(solution)/shard_map/ppermute | solution.py:12
  8.9 11.6 %collective-permute-start.1 = (bf16[2,128,512]{2,1,0:T(8,128)(2,1)}, bf16[2,128,512]{2,1,0:T(8,128)(2,1)S(1)}, u32[]{:S(2)}, u32[]{:S(2)}) collective-permute-start(bf16[2,128,512]{2,1,0:T(8,128)(2,1)} %bitcast.68), channel_id=1, source_target_pairs={{0,1},{1,2},{2,3},{3,4},{4,5},{5,6},{6,7},{7,8},{8,9},{9,10},{10,1... | collective-permute-start | bytes 786440 | tf_op jit(solution)/shard_map/ppermute | solution.py:12
  8.9 11.7 %collective-permute-start.2 = (bf16[2,128,512]{2,1,0:T(8,128)(2,1)}, bf16[2,128,512]{2,1,0:T(8,128)(2,1)S(1)}, u32[]{:S(2)}, u32[]{:S(2)}) collective-permute-start(bf16[2,128,512]{2,1,0:T(8,128)(2,1)} %bitcast.69), channel_id=1, source_target_pairs={{0,31},{1,0},{2,1},{3,2},{4,3},{5,4},{6,5},{7,6},{8,7},{9,8},{10,9... | collective-permute-start | bytes 786440 | tf_op jit(solution)/shard_map/ppermute | solution.py:12
  12.7 9.3 %collective-permute-start.3 = (bf16[2,128,512]{2,1,0:T(8,128)(2,1)}, bf16[2,128,512]{2,1,0:T(8,128)(2,1)S(1)}, u32[]{:S(2)}, u32[]{:S(2)}) collective-permute-start(bf16[2,128,512]{2,1,0:T(8,128)(2,1)} %bitcast.70), channel_id=1, source_target_pairs={{0,30},{1,31},{2,0},{3,1},{4,2},{5,3},{6,4},{7,5},{8,6},{9,7},{10,... | collective-permute-start | bytes 786440 | tf_op jit(solution)/shard_map/ppermute | solution.py:12
  22.0 2.8 copy-start.1
  24.8 3.1 copy-start.4
  24.8 3.1 copy-start.5
  122.5 17.3 %copy-start.3 = (bf16[512,512]{1,0:T(8,128)(2,1)S(1)}, bf16[512,512]{1,0:T(8,128)(2,1)}, u32[]{:S(2)}) copy-start(bf16[512,512]{1,0:T(8,128)(2,1)} %param.13) | copy-start | bytes 1572868
  122.6 8.8 %collective-permute-start.4 = (bf16[2,128,512]{2,1,0:T(8,128)(2,1)S(1)}, bf16[2,128,512]{2,1,0:T(8,128)(2,1)S(1)}, u32[]{:S(2)}, u32[]{:S(2)}) collective-permute-start(bf16[2,128,512]{2,1,0:T(8,128)(2,1)S(1)} %bitcast.78), channel_id=1, source_target_pairs={{0,30},{1,31},{2,0},{3,1},{4,2},{5,3},{6,4},{7,5},{8,6},{9,7},{10,... | collective-permute-start | bytes 786440 | tf_op jit(solution)/shard_map/ppermute | solution.py:12
  127.5 6.7 %collective-permute-start.5 = (bf16[2,128,512]{2,1,0:T(8,128)(2,1)S(1)}, bf16[2,128,512]{2,1,0:T(8,128)(2,1)S(1)}, u32[]{:S(2)}, u32[]{:S(2)}) collective-permute-start(bf16[2,128,512]{2,1,0:T(8,128)(2,1)S(1)} %bitcast.79), channel_id=1, source_target_pairs={{0,31},{1,0},{2,1},{3,2},{4,3},{5,4},{6,5},{7,6},{8,7},{9,8},{10,9... | collective-permute-start | bytes 786440 | tf_op jit(solution)/shard_map/ppermute | solution.py:12
  127.6 9.6 %collective-permute-start.6 = (bf16[2,128,512]{2,1,0:T(8,128)(2,1)S(1)}, bf16[2,128,512]{2,1,0:T(8,128)(2,1)S(1)}, u32[]{:S(2)}, u32[]{:S(2)}) collective-permute-start(bf16[2,128,512]{2,1,0:T(8,128)(2,1)S(1)} %bitcast.80), channel_id=1, source_target_pairs={{0,1},{1,2},{2,3},{3,4},{4,5},{5,6},{6,7},{7,8},{8,9},{9,10},{10,1... | collective-permute-start | bytes 786440 | tf_op jit(solution)/shard_map/ppermute | solution.py:12
  128.2 11.4 %collective-permute-start.7 = (bf16[2,128,512]{2,1,0:T(8,128)(2,1)S(1)}, bf16[2,128,512]{2,1,0:T(8,128)(2,1)S(1)}, u32[]{:S(2)}, u32[]{:S(2)}) collective-permute-start(bf16[2,128,512]{2,1,0:T(8,128)(2,1)S(1)} %bitcast.81), channel_id=1, source_target_pairs={{0,2},{1,3},{2,4},{3,5},{4,6},{5,7},{6,8},{7,9},{8,10},{9,11},{10,... | collective-permute-start | bytes 786440 | tf_op jit(solution)/shard_map/ppermute | solution.py:12
Sparse Core Ops, SparseCore 0:
  121.8 269.6 all-reduce.2
where the time goes:
time: 403 us
  waiting for transfers between devices  265 us (66%)
  other arithmetic  84.4 us (21%)
  local copies, waits for them, and re-layouts  16.1 us (4%)
  between operations  14.2 us (4%)
  matrix products  11.9 us (3%)
  starting transfers between devices  11.6 us (3%)
    psum x1, waiting for transfers between devices, local(): total_self, total_neigh = lax.psum((part_self, part_neigh), ('grp', 'feat'))  251 us
    scatter-add x1, other arithmetic, local(): jax.ops.segment_sum(contrib_flat, flat_index, num_segments=window_count)  75.4 us
    ppermute x8, waiting for transfers between devices, passed_along(): return lax.ppermute(x, axis, [(i, (i + by) % peers) for i in range(peers)])  13.8 us
    ppermute x8, starting transfers between devices, passed_along(): return lax.ppermute(x, axis, [(i, (i + by) % peers) for i in range(peers)])  11.6 us
    unnamed x23, local copies, waits for them, and re-layouts  10.9 us
  transfers between devices with their start and end apart: 9, of which 7 were waited for; matrix products, arithmetic and copies ran while one was open for 2% of the time, Pallas kernels for 0%

commit v1 on v0

--- a/solution.py
+++ b/solution.py
@@ -23,6 +23,12 @@
 def local(
     features, adj_tiles, src_block, counts, w_self, w_neigh, multiplier, bit_shift, cotangent
 ):
+
+    def build_table_all(obj):
+        for d in ("grp", "feat"):
+            obj = jax.lax.psum(obj, d)
+        return obj
+
     num_blocks = adj_tiles.shape[0]
     num_slots = adj_tiles.shape[1]
     block_len = adj_tiles.shape[2]
@@ -61,7 +67,7 @@
     ).astype(jnp.bfloat16)
     part_self = jnp.dot(features.T, grad_pre, preferred_element_type=jnp.float32)
     part_neigh = jnp.dot(aggregated.T, grad_pre, preferred_element_type=jnp.float32)
-    total_self, total_neigh = lax.psum((part_self, part_neigh), ("grp", "feat"))
+    total_self, total_neigh = build_table_all((part_self, part_neigh))
     grad_scale = 1.0 / math.sqrt(row_count * lax.axis_size("grp") * feat_count)
     own_part = jnp.dot(grad_pre, w_self.T, preferred_element_type=jnp.float32)
     back = jnp.dot(grad_pre, w_neigh.T, preferred_element_type=jnp.float32).reshape(

time: 403 us -> 259 us (0.64)
  waiting for transfers between devices: 265 us -> 118 us
    psum x1 -> x2, waiting for transfers between devices: 251 us -> 104 us  [build_table_all(): obj = jax.lax.psum(obj, d)]
  transfers between devices with their start and end apart: 9 -> 10, of which waited for: 7 -> 7; matrix products, arithmetic and copies ran while one was open for 2% -> 38% of each run, Pallas kernels for 0% -> 0%
where the time goes in v1:
time: 259 us; the launch traced here: 257 us
  waiting for transfers between devices  118 us (46%)
  other arithmetic  84.8 us (33%)
  local copies, waits for them, and re-layouts  16.1 us (6%)
  between operations  14.3 us (6%)
  matrix products  11.9 us (5%)
  starting transfers between devices  11.6 us (4%)
    psum x2, waiting for transfers between devices, build_table_all(): obj = jax.lax.psum(obj, d)  104 us
    scatter-add x1, other arithmetic, local(): jax.ops.segment_sum(contrib_flat, flat_index, num_segments=window_count)  75.9 us
    ppermute x8, waiting for transfers between devices, passed_along(): return lax.ppermute(x, axis, [(i, (i + by) % peers) for i in range(peers)])  13.9 us
    ppermute x8, starting transfers between devices, passed_along(): return lax.ppermute(x, axis, [(i, (i + by) % peers) for i in range(peers)])  11.3 us
    unnamed x23, local copies, waits for them, and re-layouts  10.9 us
  transfers between devices with their start and end apart: 10, of which 7 were waited for; matrix products, arithmetic and copies ran while one was open for 38% of the time, Pallas kernels for 0%

profile of v1, /device:TPU:2, one launch (start us, length us, event | category | flops | bytes accessed | tf_op | source)
XLA Modules:
  0.0 257.2 jit_solution(12141913314779163826)
XLA Ops:
  7.2 0.0 copy-start
  7.2 0.0 copy-start.2
  7.2 0.0 all-reduce.7.cloned.1.call-start
  7.2 1.7 collective-permute-start
  8.9 0.0 collective-permute-start.1
  8.9 3.9 %collective-permute-start.2 = (bf16[2,128,512]{2,1,0:T(8,128)(2,1)}, bf16[2,128,512]{2,1,0:T(8,128)(2,1)S(1)}, u32[]{:S(2)}, u32[]{:S(2)}) collective-permute-start(bf16[2,128,512]{2,1,0:T(8,128)(2,1)} %bitcast.69), channel_id=1, source_target_pairs={{0,31},{1,0},{2,1},{3,2},{4,3},{5,4},{6,5},{7,6},{8,7},{9,8},{10,9... | collective-permute-start | bytes 786440 | tf_op jit(solution)/shard_map/ppermute | solution.py:12
  12.7 0.4 collective-permute-start.3
  13.2 0.7 compare_and_fusion
  13.9 0.1 reshape.97
  14.0 0.7 iota_compare_fusion
  14.7 2.2 fusion.33
  16.9 0.7 exponential_multiply_fusion
  17.6 1.6 convert_reduce_fusion
  19.3 1.2 collective-permute-done.1
  20.6 1.4 collective-permute-done.3
  22.0 0.0 copy-start.1
  22.0 2.8 %gather_fusion = bf16[32,128,512]{2,1,0:T(8,128)(2,1)} fusion(bf16[10,128,512]{2,1,0:T(8,128)(2,1)S(1)} %constant_dynamic-update-slice_fusion, s32[1024]{0:T(1024)S(1)} %pad_clamp_fusion), kind=kCustom, calls=%fused_computation | custom fusion | bytes 8388736 | tf_op jit(solution)/shard_map/jit(_take)/gather | solution.py:52
  24.8 3.1 %fusion.11 = bf16[2,128,512]{2,1,0:T(8,128)(2,1)S(1)} fusion(bf16[2,16,128,512]{3,2,1,0:T(8,128)(2,1)} %bitcast.66, pred[2,16]{1,0:T(4,128)(4,1)S(1)} %get-tuple-element.12, bf16[2,16,128,128]{3,2,1,0:T(8,128)(2,1)S(1)} %copy-done.1, pred[2,16]{1,0:T(4,128)(4,1)S(1)} %iota_compare_fusion, f32[2,128]{1,0:T(2,128)S(1)} %rsqrt.7), kind=kOutput, calls=%fused_computation.12 | convolution fusion | flops 539754496 | bytes 5506112 | tf_op jit(solution)/shard_map/bkij,bkjf->bif/dot_general | solution.py:55
  28.0 1.2 multiply_convert_fusion.1
  29.2 1.3 fusion.35
  30.5 1.3 convolution_bitcast_fusion
  31.8 0.0 all-reduce.7.cloned.1.call-update
  31.8 0.2 all-reduce.5.cloned.1.call-start
  32.1 0.1 reshape.113
  32.1 0.3 fusion.34
  32.5 1.4 fusion.14
  33.9 8.1 %copy.21 = f32[4,8,128,512]{3,1,2,0:T(8,128)} copy(f32[4,8,128,512]{3,2,1,0:T(8,128)S(1)} %bitcast.65) | data formatting | bytes 16777216
  42.0 2.2 broadcast_in_dim.35
  44.2 75.9 %scatter_fusion = f32[10,65536]{1,0:T(8,128)} fusion(f32[10,65536]{1,0:T(8,128)} %broadcast_in_dim.35, s32[32]{0:T(128)S(1)} %reshape.113, f32[32,65536]{1,0:T(8,128)} %bitcast.64), kind=kCustom, calls=%fused_computation.1 | custom fusion | flops 2097152 | bytes 25165952 | tf_op jit(solution)/shard_map/scatter-add | solution.py:80
  120.1 2.4 convert_element_type.52
  122.5 0.0 all-reduce.7.cloned.1.call-done
  122.6 0.0 all-reduce.5.cloned.1.call-update
  122.6 0.8 fusion.32
  123.4 0.0 copy-start.3
  123.5 4.6 %collective-permute-start.4 = (bf16[2,128,512]{2,1,0:T(8,128)(2,1)S(1)}, bf16[2,128,512]{2,1,0:T(8,128)(2,1)S(1)}, u32[]{:S(2)}, u32[]{:S(2)}) collective-permute-start(bf16[2,128,512]{2,1,0:T(8,128)(2,1)S(1)} %bitcast.78), channel_id=1, source_target_pairs={{0,30},{1,31},{2,0},{3,1},{4,2},{5,3},{6,4},{7,5},{8,6},{9,7},{10,... | collective-permute-start | bytes 786440 | tf_op jit(solution)/shard_map/ppermute | solution.py:12
  128.1 0.1 collective-permute-start.5
  128.2 0.6 collective-permute-start.6
  128.9 0.1 collective-permute-start.7
  128.9 3.0 %collective-permute-done.4 = bf16[2,128,512]{2,1,0:T(8,128)(2,1)S(1)} collective-permute-done((bf16[2,128,512]{2,1,0:T(8,128)(2,1)S(1)}, bf16[2,128,512]{2,1,0:T(8,128)(2,1)S(1)}, u32[]{:S(2)}, u32[]{:S(2)}) %collective-permute-start.4) | collective-permute-done | bytes 262176 | tf_op jit(solution)/shard_map/ppermute | solution.py:12
  132.0 2.8 %collective-permute-done.5 = bf16[2,128,512]{2,1,0:T(8,128)(2,1)S(1)} collective-permute-done((bf16[2,128,512]{2,1,0:T(8,128)(2,1)S(1)}, bf16[2,128,512]{2,1,0:T(8,128)(2,1)S(1)}, u32[]{:S(2)}, u32[]{:S(2)}) %collective-permute-start.5) | collective-permute-done | bytes 262176 | tf_op jit(solution)/shard_map/ppermute | solution.py:12
  134.8 3.1 %collective-permute-done.6 = bf16[2,128,512]{2,1,0:T(8,128)(2,1)S(1)} collective-permute-done((bf16[2,128,512]{2,1,0:T(8,128)(2,1)S(1)}, bf16[2,128,512]{2,1,0:T(8,128)(2,1)S(1)}, u32[]{:S(2)}, u32[]{:S(2)}) %collective-permute-start.6) | collective-permute-done | bytes 262176 | tf_op jit(solution)/shard_map/ppermute | solution.py:12
  137.9 2.4 collective-permute-done.7
  140.2 0.2 fusion.17
  140.4 1.0 fusion.18
  141.4 104.5 %all-reduce.5.cloned.1.call-done = (f32[512,512]{0,1:T(8,128)}, f32[512,512]{0,1:T(8,128)}) async-done(((f32[512,512]{0,1:T(8,128)}, f32[512,512]{0,1:T(8,128)}), (f32[512,512]{0,1:T(8,128)}, f32[512,512]{0,1:T(8,128)})) %all-reduce.5.cloned.1.call-update) | async-done | bytes 2097168 | tf_op jit(solution)/shard_map/psum | solution.py:29
  245.9 1.8 broadcast_multiply_fusion
  247.7 1.3 copy.15
  249.1 1.3 copy.16
  (22 shorter events, 0.2 us)
Async XLA Ops:
  7.2 20.8 %copy-start = (bf16[512,512]{1,0:T(8,128)(2,1)S(1)}, bf16[512,512]{1,0:T(8,128)(2,1)}, u32[]{:S(2)}) copy-start(bf16[512,512]{1,0:T(8,128)(2,1)} %param.14) | copy-start | bytes 1572868
  7.2 13.3 %copy-start.2 = (bf16[256,512]{1,0:T(8,128)(2,1)S(1)}, bf16[256,512]{1,0:T(8,128)(2,1)}, u32[]{:S(2)}) copy-start(bf16[256,512]{1,0:T(8,128)(2,1)} %param.9) | copy-start | bytes 786436
  7.2 115.4 %all-reduce.7.cloned.1.call-start = ((), (), s32[]{:S(2)}) async-start(), calls=%async_computation.1 | async-start | bytes 4194304 | tf_op jit(solution)/shard_map/psum | solution.py:29
  7.2 12.0 %collective-permute-start = (bf16[2,128,512]{2,1,0:T(8,128)(2,1)}, bf16[2,128,512]{2,1,0:T(8,128)(2,1)S(1)}, u32[]{:S(2)}, u32[]{:S(2)}) collective-permute-start(bf16[2,128,512]{2,1,0:T(8,128)(2,1)} %bitcast.67), channel_id=1, source_target_pairs={{0,2},{1,3},{2,4},{3,5},{4,6},{5,7},{6,8},{7,9},{8,10},{9,11},{10,... | collective-permute-start | bytes 786440 | tf_op jit(solution)/shard_map/ppermute | solution.py:12
  8.9 11.6 %collective-permute-start.1 = (bf16[2,128,512]{2,1,0:T(8,128)(2,1)}, bf16[2,128,512]{2,1,0:T(8,128)(2,1)S(1)}, u32[]{:S(2)}, u32[]{:S(2)}) collective-permute-start(bf16[2,128,512]{2,1,0:T(8,128)(2,1)} %bitcast.68), channel_id=1, source_target_pairs={{0,1},{1,2},{2,3},{3,4},{4,5},{5,6},{6,7},{7,8},{8,9},{9,10},{10,1... | collective-permute-start | bytes 786440 | tf_op jit(solution)/shard_map/ppermute | solution.py:12
  8.9 11.7 %collective-permute-start.2 = (bf16[2,128,512]{2,1,0:T(8,128)(2,1)}, bf16[2,128,512]{2,1,0:T(8,128)(2,1)S(1)}, u32[]{:S(2)}, u32[]{:S(2)}) collective-permute-start(bf16[2,128,512]{2,1,0:T(8,128)(2,1)} %bitcast.69), channel_id=1, source_target_pairs={{0,31},{1,0},{2,1},{3,2},{4,3},{5,4},{6,5},{7,6},{8,7},{9,8},{10,9... | collective-permute-start | bytes 786440 | tf_op jit(solution)/shard_map/ppermute | solution.py:12
  12.7 9.3 %collective-permute-start.3 = (bf16[2,128,512]{2,1,0:T(8,128)(2,1)}, bf16[2,128,512]{2,1,0:T(8,128)(2,1)S(1)}, u32[]{:S(2)}, u32[]{:S(2)}) collective-permute-start(bf16[2,128,512]{2,1,0:T(8,128)(2,1)} %bitcast.70), channel_id=1, source_target_pairs={{0,30},{1,31},{2,0},{3,1},{4,2},{5,3},{6,4},{7,5},{8,6},{9,7},{10,... | collective-permute-start | bytes 786440 | tf_op jit(solution)/shard_map/ppermute | solution.py:12
  22.0 2.8 %copy-start.1 = (bf16[2,16,128,128]{3,2,1,0:T(8,128)(2,1)S(1)}, bf16[2,16,128,128]{3,2,1,0:T(8,128)(2,1)}, u32[]{:S(2)}) copy-start(bf16[2,16,128,128]{3,2,1,0:T(8,128)(2,1)} %param.10) | copy-start | bytes 3145732
  24.8 3.1 %copy-start.4 = (f32[256,512]{1,0:T(8,128)S(1)}, f32[256,512]{1,0:T(8,128)}, u32[]{:S(2)}) copy-start(f32[256,512]{1,0:T(8,128)} %fusion.33) | copy-start | bytes 1572868
  24.8 3.1 %copy-start.5 = (bf16[256,512]{1,0:T(8,128)(2,1)S(1)}, bf16[256,512]{1,0:T(8,128)(2,1)}, u32[]{:S(2)}) copy-start(bf16[256,512]{1,0:T(8,128)(2,1)} %param.17) | copy-start | bytes 786436
  31.8 214.1 %all-reduce.5.cloned.1.call-start = ((), (), s32[]{:S(2)}) async-start(), calls=%async_computation | async-start | bytes 4194304 | tf_op jit(solution)/shard_map/psum | solution.py:29
  123.4 17.0 %copy-start.3 = (bf16[512,512]{1,0:T(8,128)(2,1)S(1)}, bf16[512,512]{1,0:T(8,128)(2,1)}, u32[]{:S(2)}) copy-start(bf16[512,512]{1,0:T(8,128)(2,1)} %param.13) | copy-start | bytes 1572868
  123.5 8.5 %collective-permute-start.4 = (bf16[2,128,512]{2,1,0:T(8,128)(2,1)S(1)}, bf16[2,128,512]{2,1,0:T(8,128)(2,1)S(1)}, u32[]{:S(2)}, u32[]{:S(2)}) collective-permute-start(bf16[2,128,512]{2,1,0:T(8,128)(2,1)S(1)} %bitcast.78), channel_id=1, source_target_pairs={{0,30},{1,31},{2,0},{3,1},{4,2},{5,3},{6,4},{7,5},{8,6},{9,7},{10,... | collective-permute-start | bytes 786440 | tf_op jit(solution)/shard_map/ppermute | solution.py:12
  128.1 6.7 %collective-permute-start.5 = (bf16[2,128,512]{2,1,0:T(8,128)(2,1)S(1)}, bf16[2,128,512]{2,1,0:T(8,128)(2,1)S(1)}, u32[]{:S(2)}, u32[]{:S(2)}) collective-permute-start(bf16[2,128,512]{2,1,0:T(8,128)(2,1)S(1)} %bitcast.79), channel_id=1, source_target_pairs={{0,31},{1,0},{2,1},{3,2},{4,3},{5,4},{6,5},{7,6},{8,7},{9,8},{10,9... | collective-permute-start | bytes 786440 | tf_op jit(solution)/shard_map/ppermute | solution.py:12
  128.2 9.6 %collective-permute-start.6 = (bf16[2,128,512]{2,1,0:T(8,128)(2,1)S(1)}, bf16[2,128,512]{2,1,0:T(8,128)(2,1)S(1)}, u32[]{:S(2)}, u32[]{:S(2)}) collective-permute-start(bf16[2,128,512]{2,1,0:T(8,128)(2,1)S(1)} %bitcast.80), channel_id=1, source_target_pairs={{0,1},{1,2},{2,3},{3,4},{4,5},{5,6},{6,7},{7,8},{8,9},{9,10},{10,1... | collective-permute-start | bytes 786440 | tf_op jit(solution)/shard_map/ppermute | solution.py:12
  128.9 11.4 %collective-permute-start.7 = (bf16[2,128,512]{2,1,0:T(8,128)(2,1)S(1)}, bf16[2,128,512]{2,1,0:T(8,128)(2,1)S(1)}, u32[]{:S(2)}, u32[]{:S(2)}) collective-permute-start(bf16[2,128,512]{2,1,0:T(8,128)(2,1)S(1)} %bitcast.81), channel_id=1, source_target_pairs={{0,2},{1,3},{2,4},{3,5},{4,6},{5,7},{6,8},{7,9},{8,10},{9,11},{10,... | collective-permute-start | bytes 786440 | tf_op jit(solution)/shard_map/ppermute | solution.py:12
Sparse Core Ops, SparseCore 0:
  31.9 86.4 all-reduce.6
  122.7 123.1 all-reduce.4
